TPU v7x, 32 devices: a whole 2x2x4 slice. The times are simulated.
32 devices in a mesh: dp: 8 (over y, x, core), fsdp: 4 (over z).
Axes of the slice: x: 2, y: 2, z: 4, core: 2. Of those that a mesh axis runs over, the one named last changes fastest.
Arguments:
- img_emb: bfloat16 [1024, 1024], P(('dp', 'fsdp')), may hold values from -0.25 to 0.25
- txt_emb: bfloat16 [1024, 1024], P(('dp', 'fsdp')), may hold values from -0.25 to 0.25
- img_ids: int32 [1024], P(('dp', 'fsdp')), may hold values from 0 to 1023
- txt_ids: int32 [1024], P(('dp', 'fsdp')), may hold values from 0 to 1023
- temp_log: float32 [1], replicated, may hold values from 1.5 to 2.5
- logit_bias: float32 [1], replicated, may hold values from -6 to -2
- block_in: bfloat16 [2048, 3072], P(('dp', 'fsdp')), may hold values from -6 to 6
- dw_kernel: float32 [49, 3072], replicated, may hold values from -0.875 to 0.875
- ln_gain: float32 [3072], replicated, may hold values from 0.5 to 1.5
- ln_bias: float32 [3072], replicated, may hold values from -3 to 3
- w_up: bfloat16 [3072, 6144], P(None, 'fsdp'), may hold values from -0.109375 to 0.109375
- w_down: bfloat16 [6144, 3072], P('fsdp'), may hold values from -0.078125 to 0.078125
- layer_scale: float32 [3072], replicated, may hold values from 0.1 to 1
- head_gain: float32 [3072], replicated, may hold values from 0.5 to 1.5
- head_bias: float32 [3072], replicated, may hold values from -3 to 3
- w_proj: bfloat16 [3072, 1024], replicated, may hold values from -0.109375 to 0.109375
Outputs:
- img_grad: float32 [1024, 1024], P(('dp', 'fsdp'))
- txt_grad: float32 [1024, 1024], P(('dp', 'fsdp'))
- w_up_grad: float32 [3072, 6144], P('dp', 'fsdp')
- w_down_grad: float32 [6144, 3072], P('fsdp', 'dp')
All inputs are finite; a program needn't handle non-finite values.
Results may differ from a plain program's by a relative error of at most 0.02.
Values may be sent and summed in bfloat16 or wider, within the bound.
A program may use at most 128 MiB of HBM per device.

v0:
```python
import jax
import jax.numpy as jnp
from jax import lax
from jax.sharding import PartitionSpec as P

KERNEL = 7
SIDE = 8


def unit_rows(matrix):
    values = matrix.astype(jnp.float32)
    length = jnp.sqrt(jnp.sum(values * values, axis=1, keepdims=True) + 1e-06)
    return (values / length, length)


def back_unit(gradient, unit_part, length):
    inner_prod = jnp.sum(unit_part * gradient, axis=1, keepdims=True)
    return (gradient - unit_part * inner_prod) / length


def depthwise(pictures, kernel):
    reach = KERNEL // 2
    padded = jnp.pad(pictures, ((0, 0), (reach, reach), (reach, reach), (0, 0)))
    summed = jnp.zeros_like(pictures)
    for above in range(KERNEL):
        for across in range(KERNEL):
            summed = (
                summed
                + kernel[above * KERNEL + across]
                * padded[:, above : above + SIDE, across : across + SIDE, :]
            )
    return summed


def layer_norm(values, gain_vec, bias_vec):
    centre = jnp.mean(values, axis=-1, keepdims=True)
    centred = values - centre
    inverse = 1.0 / jnp.sqrt(jnp.mean(centred * centred, axis=-1, keepdims=True) + 1e-06)
    normal = centred * inverse
    return (normal * gain_vec + bias_vec, normal, inverse)


def head_back(patch_means, block_mean, image_sum, layer_scale, head_gain, head_bias, w_proj):
    pooled = patch_means.astype(jnp.float32) + layer_scale * block_mean
    head_out, head_norm, inverse = layer_norm(pooled, head_gain, head_bias)
    embed = jnp.dot(head_out.astype(jnp.bfloat16), w_proj, preferred_element_type=jnp.float32)
    embed_unit, embed_len = unit_rows(embed)
    embed_grad = back_unit(image_sum, embed_unit, embed_len).astype(jnp.bfloat16)
    head_grad = jnp.dot(embed_grad, w_proj.T, preferred_element_type=jnp.float32)
    norm_grad = head_grad * head_gain
    pool_grad = inverse * (
        norm_grad
        - jnp.mean(norm_grad, axis=1, keepdims=True)
        - head_norm * jnp.mean(norm_grad * head_norm, axis=1, keepdims=True)
    )
    return (layer_scale * pool_grad / (SIDE * SIDE)).astype(jnp.bfloat16)


def id_columns(ids):
    codes = jnp.stack([ids // 256, ids % 256], axis=1).astype(jnp.bfloat16)
    return jnp.pad(codes, ((0, 0), (0, 126)))


def split_two(values):
    high = lax.reduce_precision(values, 8, 7)
    low = values - high
    return (high.astype(jnp.bfloat16), low.astype(jnp.bfloat16))


def pair_tile_coded(images, image_codes, text_rows, text_codes, temper, offset):
    scores = jnp.dot(images, text_rows.T, preferred_element_type=jnp.float32)
    logits = temper * scores + offset
    same = (image_codes[:, 0][:, None] == text_codes[:, 0][None, :]) & (
        image_codes[:, 1][:, None] == text_codes[:, 1][None, :]
    )
    labels = jnp.where(same, 1.0, -1.0)
    weights = (temper * -labels * jax.nn.sigmoid(-labels * logits)).astype(jnp.bfloat16)
    image_part = jnp.dot(weights, text_rows, preferred_element_type=jnp.float32)
    text_part = jnp.dot(weights.T, images, preferred_element_type=jnp.float32)
    return (image_part, text_part)


def on_device(
    img_emb,
    txt_emb,
    img_ids,
    txt_ids,
    temp_log,
    logit_bias,
    block_in,
    dw_kernel,
    ln_gain,
    ln_bias,
    w_up,
    w_down,
    layer_scale,
    head_gain,
    head_bias,
    w_proj,
):
    channels = block_in.shape[1]
    hid_width = w_up.shape[1]
    embed_width = img_emb.shape[1]
    pairs = img_emb.shape[0]
    patches = SIDE * SIDE
    n_dp, n_fsdp = (lax.axis_size("dp"), lax.axis_size("fsdp"))
    temper = jnp.exp(temp_log[0])
    offset = logit_bias[0]
    img_unit, img_len = unit_rows(img_emb)
    txt_unit, txt_len = unit_rows(txt_emb)
    img_b = jnp.concatenate([img_unit.astype(jnp.bfloat16), id_columns(img_ids)], axis=1)
    txt_b = jnp.concatenate([txt_unit.astype(jnp.bfloat16), id_columns(txt_ids)], axis=1)
    group_img = lax.all_gather(img_b, "fsdp", axis=0, tiled=True)
    column_txt = lax.all_gather(txt_b, "dp", axis=0, tiled=True)
    pictures = block_in.astype(jnp.float32).reshape(1, SIDE, SIDE, channels)
    mixed_rows = depthwise(pictures, dw_kernel).reshape(patches, channels)
    normed = layer_norm(mixed_rows, ln_gain, ln_bias)[0].astype(jnp.bfloat16)
    patch_means = jnp.mean(pictures, axis=(1, 2)).astype(jnp.bfloat16)
    group_normed = lax.all_gather(normed, "fsdp", axis=0, tiled=True)
    image_part, text_part = pair_tile_coded(
        group_img[:, :embed_width],
        group_img[:, embed_width:],
        column_txt[:, :embed_width],
        column_txt[:, embed_width:],
        temper,
        offset,
    )
    hidden = jnp.dot(group_normed, w_up, preferred_element_type=jnp.float32)
    activated, pullback = jax.vjp(jax.nn.gelu, hidden)
    slope = pullback(jnp.ones_like(hidden))[0].astype(jnp.bfloat16)
    active_total = jnp.sum(
        activated.astype(jnp.bfloat16).astype(jnp.float32).reshape(n_fsdp, patches, hid_width),
        axis=1,
    )
    high, low = split_two(active_total / patches)
    both = jnp.dot(jnp.concatenate([high, low]), w_down, preferred_element_type=jnp.float32)
    partial_mean = both[:n_fsdp] + both[n_fsdp:]
    mean_rows = channels // embed_width
    fill = -(pairs + mean_rows) % 16
    terms = jnp.concatenate(
        [
            image_part.astype(jnp.bfloat16).reshape(n_fsdp, pairs, embed_width),
            partial_mean.astype(jnp.bfloat16).reshape(n_fsdp, mean_rows, embed_width),
            jnp.zeros((n_fsdp, fill, embed_width), jnp.bfloat16),
        ],
        axis=1,
    ).reshape(-1, embed_width)
    term_sum = lax.psum_scatter(terms, "fsdp", scatter_dimension=0, tiled=True).astype(jnp.float32)
    image_sum = term_sum[:pairs]
    block_mean = term_sum[pairs : pairs + mean_rows].reshape(1, channels)
    all_slope = lax.all_gather(slope, "dp", axis=0, tiled=True)
    own_normed = lax.all_to_all(group_normed, "dp", split_axis=1, concat_axis=0, tiled=True)
    all_active = lax.all_gather(active_total, "dp", axis=0, tiled=True)
    grad_row = head_back(
        patch_means, block_mean, image_sum[:1], layer_scale, head_gain, head_bias, w_proj
    )
    all_grad = lax.all_gather(grad_row, ("dp", "fsdp"), axis=0, tiled=True)
    row_down = jnp.dot(all_grad, w_down.T, preferred_element_type=jnp.float32)
    hid_grad = (
        (
            all_slope.reshape(n_dp * n_fsdp, patches, hid_width).astype(jnp.float32)
            * row_down[:, None, :]
        )
        .astype(jnp.bfloat16)
        .reshape(-1, hid_width)
    )
    w_up_grad = lax.dot_general(
        own_normed, hid_grad, (((0,), (0,)), ((), ())), preferred_element_type=jnp.float32
    )
    share = channels // n_dp
    own_grad = lax.dynamic_slice_in_dim(all_grad, lax.axis_index("dp") * share, share, 1)
    high, low = split_two(all_active)
    w_down_grad = lax.dot_general(
        jnp.concatenate([high, low]),
        jnp.concatenate([own_grad, own_grad]),
        (((0,), (0,)), ((), ())),
        preferred_element_type=jnp.float32,
    )
    text_sum = lax.psum_scatter(
        text_part.astype(jnp.bfloat16), "dp", scatter_dimension=0, tiled=True
    ).astype(jnp.float32)
    img_grad = back_unit(image_sum, img_unit, img_len)
    txt_grad = back_unit(text_sum, txt_unit, txt_len)
    return (img_grad, txt_grad, w_up_grad, w_down_grad)


def solution(mesh):
    in_specs = (
        P(("dp", "fsdp"), None),
        P(("dp", "fsdp"), None),
        P(("dp", "fsdp")),
        P(("dp", "fsdp")),
        P(),
        P(),
        P(("dp", "fsdp"), None),
        P(),
        P(),
        P(),
        P(None, "fsdp"),
        P("fsdp", None),
        P(),
        P(),
        P(),
        P(),
    )
    out_specs = (P(("dp", "fsdp"), None), P(("dp", "fsdp"), None), P("dp", "fsdp"), P("fsdp", "dp"))
    return jax.shard_map(
        on_device, mesh=mesh, in_specs=in_specs, out_specs=out_specs, check_vma=False
    )
```

profile of v0, /device:TPU:0, one launch (start us, length us, event | category | flops | bytes accessed | tf_op | source)
XLA Modules:
  0.0 232.2 jit_solution(10827086138796158804)
XLA Ops:
  8.0 1.5 fusion.163
  9.5 2.1 fusion.161
  11.6 1.9 fusion.162
  14.6 5.5 %fusion.159 = (f32[8,8]{1,0:T(8,128)S(1)}, f32[1,8,8,3072]{3,2,1,0:T(8,128)S(1)}) fusion(f32[3072]{0:T(1024)S(1)} %bitcast.123, f32[3072]{0:T(1024)S(1)} %bitcast.124, f32[3072]{0:T(1024)S(1)} %bitcast.127, f32[3072]{0:T(1024)S(1)} %bitcast.128, f32[3072]{0:T(1024)S(1)} %bitcast.129, f32[3072]{0:T(1024)S(1)} %bitcast.130, f32[3072]{0:T(1024)S(1)} %bitcast.131, ...), kind=kLoop, calls=%fused_computation.268 | loop fusion | flops 19267520 | bytes 2175232 | tf_op jit(solution)/shard_map/reduce_sum | solution.py:36
  23.5 17.6 %all_gather.18 = bf16[128,1152]{1,0:T(8,128)(2,1)S(1)} all-gather(bf16[32,1152]{1,0:T(8,128)(2,1)S(1)} %fusion.131), channel_id=1, replica_groups=mesh['dp'=8,'fsdp'=4] {'fsdp'}, dimensions={0}, use_global_device_ids=true | all-gather | bytes 368640 | tf_op jit(solution)/shard_map/all_gather | solution.py:113
  41.5 10.1 %all_gather.19 = bf16[256,1152]{1,0:T(8,128)(2,1)S(1)} all-gather(bf16[32,1152]{1,0:T(8,128)(2,1)S(1)} %fusion.132), channel_id=1, replica_groups=mesh['dp'=8,'fsdp'=4] {'dp'}, dimensions={0}, use_global_device_ids=true | all-gather | bytes 663552 | tf_op jit(solution)/shard_map/all_gather | solution.py:114
  52.1 1.1 convolution_convert_fusion
  53.6 9.8 %all-gather.5.cloned.1.call-done = bf16[256,3072]{1,0:T(8,128)(2,1)} async-done(((bf16[64,3072]{1,0:T(8,128)(2,1)}), bf16[256,3072]{1,0:T(8,128)(2,1)}) %all-gather.5.cloned.1.call-update) | async-done | bytes 1572880 | tf_op jit(solution)/shard_map/all_gather | solution.py:119
  63.4 6.0 %convert_reduce_fusion = (f32[4,1536]{1,0:T(4,128)S(1)}, f32[256,1536]{1,0:T(8,128)S(1)}) fusion(bf16[256,3072]{1,0:T(8,128)(2,1)} %all-gather.5.cloned.1.call-done, bf16[3072,1536]{1,0:T(8,128)(2,1)} %param.26), kind=kOutput, calls=%fused_computation.59 | convolution fusion | flops 2420238336 | bytes 12607488 | tf_op jit(solution)/shard_map/dot_general | solution.py:128
  70.0 5.0 %fusion.138 = f32[8,3072]{1,0:T(8,128)S(1)} fusion(bf16[1536,3072]{1,0:T(8,128)(2,1)} %param.27, bf16[4,1536]{1,0:T(4,128)(2,1)S(1)} %get-tuple-element.67, bf16[4,1536]{1,0:T(4,128)(2,1)S(1)} %get-tuple-element.66), kind=kOutput, calls=%fused_computation.217 | convolution fusion | flops 75546624 | bytes 9560064 | tf_op jit(solution)/shard_map/dot_general | solution.py:136
  76.0 1.9 fusion.7
  78.0 9.9 %reduce-scatter.5.cloned.1.call-done = bf16[32,1024]{1,0:T(8,128)(2,1)} async-done(((bf16[256,1024]{1,0:T(8,128)(2,1)}), bf16[32,1024]{1,0:T(8,128)(2,1)}) %reduce-scatter.5.cloned.1.call-update) | async-done | bytes 65552 | tf_op jit(solution)/shard_map/reduce_scatter | solution.py:179
  87.9 1.1 fusion.129
  89.0 1.6 fusion.130
  90.6 1.6 copy.43
  92.2 3.7 %all-to-all-start = ((bf16[256,8,384]{0,2,1:T(8,128)(2,1)}), bf16[256,8,384]{0,2,1:T(8,128)(2,1)S(1)}, u32[]{:S(2)}, u32[]{:S(2)}) async-start(bf16[256,8,384]{0,2,1:T(8,128)(2,1)} %bitcast.61), calls=%async_computation.2 | async-start | bytes 3145728 | tf_op jit(solution)/shard_map/all_to_all | solution.py:152
  95.9 24.4 %all-gather.1 = f32[8,4,1536]{2,1,0:T(4,128)S(1)} all-gather(f32[1,4,1536]{2,1,0:T(4,128)S(1)} %bitcast.109), channel_id=1, replica_groups=mesh['dp'=8,'fsdp'=4] {'dp'}, dimensions={0}, use_global_device_ids=true | all-gather | bytes 221184 | tf_op jit(solution)/shard_map/all_gather | solution.py:153
  123.9 3.7 %fusion.164 = f32[1,1024]{1,0:T(1,128)S(1)} fusion(bf16[3072,1]{0,1:T(2,128)(2,1)S(1)} %reshape.344, bf16[3072,1024]{1,0:T(8,128)(2,1)} %param.31), kind=kOutput, calls=%fused_computation.272 | convolution fusion | flops 6291456 | bytes 6301696 | tf_op jit(solution)/shard_map/dot_general | solution.py:46
  130.2 4.5 %fusion.142 = f32[1,3072]{1,0:T(1,128)S(1)} fusion(bf16[3072,1024]{1,0:T(8,128)(2,1)} %param.31, f32[1,1024]{1,0:T(1,128)S(1)} %bitcast.164, f32[48,1024]{1,0:T(8,128)S(1)} %convert_element_type.103, f32[]{:T(128)S(6)} %sqrt.33), kind=kOutput, calls=%fused_computation.228 | convolution fusion | flops 6294528 | bytes 6311940 | tf_op jit(solution)/shard_map/dot_general | solution.py:49
  136.7 69.3 %all-gather = bf16[98304]{0:T(1024)(128)(2,1)S(1)} all-gather(bf16[3072]{0:T(1024)(128)(2,1)S(1)} %multiply_convert_fusion.1), channel_id=2, replica_groups=mesh['dp'=8,'fsdp'=4] {'dp','fsdp'}, dimensions={0}, use_global_device_ids=true | all-gather | bytes 202752 | tf_op jit(solution)/shard_map/all_gather | solution.py:157
  206.4 1.9 fusion.121
  209.1 6.5 %fusion.165 = f32[32,1536]{1,0:T(8,128)S(1)} fusion(bf16[32,3072]{1,0:T(8,128)(2,1)S(1)} %reshape.341, bf16[1536,3072]{1,0:T(8,128)(2,1)} %param.27), kind=kOutput, calls=%fused_computation.273 | convolution fusion | flops 301989888 | bytes 9830400 | tf_op jit(solution)/shard_map/dot_general | solution.py:158
  216.5 4.0 %fusion = bf16[2048,1536]{1,0:T(8,128)(2,1)S(1)} fusion(bf16[2048,1536]{1,0:T(8,128)(2,1)} %all-gather.7.cloned.1.call-done, f32[32,1536]{1,0:T(8,128)S(1)} %fusion.165), kind=kLoop, calls=%fused_computation.49 | loop fusion | flops 9437184 | bytes 12779520 | tf_op jit(solution)/shard_map/convert_element_type | solution.py:164
  220.5 4.1 %fusion.166 = f32[384,1536]{1,0:T(8,128)} fusion(bf16[2048,384]{1,0:T(8,128)(2,1)S(1)} %bitcast.105, bf16[2048,1536]{1,0:T(8,128)(2,1)S(1)} %fusion), kind=kOutput, calls=%fused_computation.274 | convolution fusion | flops 2415919104 | bytes 10223616 | tf_op jit(solution)/shard_map/dot_general | solution.py:167
  (93 shorter events, 12.6 us)
Async XLA Ops:
  8.0 55.4 %all-gather.5.cloned.1.call-start = ((), (), s32[]{:S(2)}) async-start(), calls=%async_computation.3 | async-start | bytes 1966080 | tf_op jit(solution)/shard_map/all_gather | solution.py:119
  14.6 6.0 %copy-start.10 = (f32[3072]{0:T(1024)S(1)}, f32[3072]{0:T(1024)}, u32[]{:S(2)}) copy-start(f32[3072]{0:T(1024)} %param.25) | copy-start | bytes 36868
  14.6 6.0 %copy-start.11 = (f32[3072]{0:T(1024)S(1)}, f32[3072]{0:T(1024)}, u32[]{:S(2)}) copy-start(f32[3072]{0:T(1024)} %param.24) | copy-start | bytes 36868
  20.1 2.8 %copy-start.2 = (bf16[32,1024]{1,0:T(8,128)(2,1)S(1)}, bf16[32,1024]{1,0:T(8,128)(2,1)}, u32[]{:S(2)}) copy-start(bf16[32,1024]{1,0:T(8,128)(2,1)} %param.16) | copy-start | bytes 196612
  20.1 2.9 %copy-start.13 = (s32[32]{0:T(128)S(1)}, s32[32]{0:T(128)}, u32[]{:S(2)}) copy-start(s32[32]{0:T(128)} %param.18) | copy-start | bytes 388
  20.1 2.9 %copy-start.14 = (s32[32]{0:T(128)S(1)}, s32[32]{0:T(128)}, u32[]{:S(2)}) copy-start(s32[32]{0:T(128)} %param.19) | copy-start | bytes 388
  20.2 21.0 %copy-start.4 = (bf16[32,1024]{1,0:T(8,128)(2,1)S(1)}, bf16[32,1024]{1,0:T(8,128)(2,1)}, u32[]{:S(2)}) copy-start(bf16[32,1024]{1,0:T(8,128)(2,1)} %param.17) | copy-start | bytes 196612
  21.5 66.4 %reduce-scatter.5.cloned.1.call-start = ((), (), s32[]{:S(2)}) async-start(), calls=%async_computation.5 | async-start | bytes 589824 | tf_op jit(solution)/shard_map/reduce_scatter | solution.py:179
  53.2 67.3 %reduce-scatter.3.cloned.1.call-start = ((), (), s32[]{:S(2)}) async-start(), calls=%async_computation.4 | async-start | bytes 491520 | tf_op jit(solution)/shard_map/reduce_scatter | solution.py:148
  69.4 0.6 copy-start.6
  76.0 140.6 %all-gather.7.cloned.1.call-start = ((), (), s32[]{:S(2)}) async-start(), calls=%async_computation.6 | async-start | bytes 7077888 | tf_op jit(solution)/shard_map/all_gather | solution.py:151
  76.0 1.9 copy-start.1
  76.0 14.6 %copy-start = (bf16[256,3072]{1,0:T(8,128)(2,1)S(1)}, bf16[256,3072]{1,0:T(8,128)(2,1)}, u32[]{:S(2)}) copy-start(bf16[256,3072]{1,0:T(8,128)(2,1)} %all-gather.5.cloned.1.call-done) | copy-start | bytes 4718596
  92.2 3.7 %copy-start.7 = (f32[4,1536]{1,0:T(4,128)S(1)}, f32[4,1536]{1,0:T(4,128)}, u32[]{:S(2)}) copy-start(f32[4,1536]{1,0:T(4,128)} %copy-done.6) | copy-start | bytes 73732
  92.2 29.1 %copy-start.9 = (f32[3072]{0:T(1024)S(1)}, f32[3072]{0:T(1024)}, u32[]{:S(2)}) copy-start(f32[3072]{0:T(1024)} %param.28) | copy-start | bytes 36868
  92.2 31.6 %copy-start.8 = (f32[3072]{0:T(1024)S(1)}, f32[3072]{0:T(1024)}, u32[]{:S(2)}) copy-start(f32[3072]{0:T(1024)} %param.29) | copy-start | bytes 36868
  92.2 31.6 %copy-start.12 = (f32[3072]{0:T(1024)S(1)}, f32[3072]{0:T(1024)}, u32[]{:S(2)}) copy-start(f32[3072]{0:T(1024)} %param.30) | copy-start | bytes 36868
  92.2 123.4 %all-to-all-start = ((bf16[256,8,384]{0,2,1:T(8,128)(2,1)}), bf16[256,8,384]{0,2,1:T(8,128)(2,1)S(1)}, u32[]{:S(2)}, u32[]{:S(2)}) async-start(bf16[256,8,384]{0,2,1:T(8,128)(2,1)} %bitcast.61), calls=%async_computation.2 | async-start | bytes 3145728 | tf_op jit(solution)/shard_map/all_to_all | solution.py:152
  123.9 5.1 %copy-start.5 = (bf16[48,1024]{1,0:T(8,128)(2,1)S(1)}, bf16[48,1024]{1,0:T(8,128)(2,1)}, u32[]{:S(2)}) copy-start(bf16[48,1024]{1,0:T(8,128)(2,1)} %reduce-scatter.3.cloned.1.call-done) | copy-start | bytes 294916
  130.2 76.0 %copy-start.3 = (bf16[32,1024]{1,0:T(8,128)(2,1)S(1)}, bf16[32,1024]{1,0:T(8,128)(2,1)}, u32[]{:S(2)}) copy-start(bf16[32,1024]{1,0:T(8,128)(2,1)} %param.16) | copy-start | bytes 196612
Sparse Core Ops, SparseCore 0:
  21.7 41.7 all-gather.4
Sparse Core Ops, SparseCore 1:
  53.3 34.5 reduce-scatter.4
  90.1 20.9 reduce-scatter.2
  112.7 43.7 all-gather.6
where the time goes:
time: 233 us; the launch traced here: 232 us
  blocking collectives  121 us (52%)
  matrix products  33.5 us (14%)
  other arithmetic  22.5 us (10%)
  between operations  20.8 us (9%)
  waiting for transfers between devices  19.8 us (8%)
  local copies, waits for them, and re-layouts  10.3 us (4%)
  starting transfers between devices  3.9 us (2%)
    all_gather x1, blocking collectives, on_device(): all_grad = lax.all_gather(grad_row, ('dp', 'fsdp'), axis=0, tiled=True)  69.3 us
    all_gather x1, blocking collectives, on_device(): all_active = lax.all_gather(active_total, 'dp', axis=0, tiled=True)  24.4 us
    all_gather x1, blocking collectives, on_device(): group_img = lax.all_gather(img_b, 'fsdp', axis=0, tiled=True)  17.6 us
    all_gather x1, blocking collectives, on_device(): column_txt = lax.all_gather(txt_b, 'dp', axis=0, tiled=True)  10.1 us
    reduce_scatter x1, waiting for transfers between devices, on_device(): lax.psum_scatter(text_part.astype(jnp.bfloat16), 'dp', scatter_dimension=...  9.87 us
    all_gather x1, waiting for transfers between devices, on_device(): group_normed = lax.all_gather(normed, 'fsdp', axis=0, tiled=True)  9.79 us
    dot_general x1, matrix products, on_device(): row_down = jnp.dot(all_grad, w_down.T, preferred_element_type=jnp.float32)  6.54 us
    reduce_sum x2, other arithmetic, layer_norm(): centre = jnp.mean(values, axis=-1, keepdims=True)  6.11 us
  transfers between devices with their start and end apart: 5, of which 2 were waited for; matrix products, arithmetic and copies ran while one was open for 19% of the time, Pallas kernels for 0%

commit v1 on v0

--- a/solution.py
+++ b/solution.py
@@ -5,6 +5,24 @@
 
 KERNEL = 7
 SIDE = 8
+
+
+def in_order(tiles, dim):
+    tiles = jnp.moveaxis(tiles, 0, dim)
+    dims = tiles.shape
+    return tiles.reshape(*dims[:dim], dims[dim] * dims[dim + 1], *dims[dim + 2 :])
+
+
+def collected_by_bits(x, axis):
+    peers = lax.axis_size(axis)
+    blocks = x[None]
+    for level in range(peers.bit_length() - 1):
+        bit = 1 << level
+        theirs = lax.ppermute(blocks, axis, [(i, i ^ bit) for i in range(peers)])
+        both = jnp.stack([blocks, theirs])
+        upper = lax.axis_index(axis) >> level & 1
+        blocks = jnp.where(upper == 0, both, both[::-1]).reshape(-1, *x.shape)
+    return blocks
 
 
 def unit_rows(matrix):
@@ -154,7 +172,7 @@
     grad_row = head_back(
         patch_means, block_mean, image_sum[:1], layer_scale, head_gain, head_bias, w_proj
     )
-    all_grad = lax.all_gather(grad_row, ("dp", "fsdp"), axis=0, tiled=True)
+    all_grad = in_order(collected_by_bits(grad_row, ("dp", "fsdp")), 0)
     row_down = jnp.dot(all_grad, w_down.T, preferred_element_type=jnp.float32)
     hid_grad = (
         (

time: 233 us -> 211 us (0.906)
  blocking collectives: 121 us -> 66.5 us
  waiting for transfers between devices: 19.8 us -> 50.2 us
  starting transfers between devices: 3.9 us -> 7.04 us
    all_gather x1 -> x0, blocking collectives: 69.3 us -> none  [on_device(): all_grad = lax.all_gather(grad_row, ('dp', 'fsdp'), axis=0, tiled=True)]
    reduce_scatter x1, waiting for transfers between devices: 0.03 us -> 22.6 us  [on_device(): lax.psum_scatter(terms, 'fsdp', scatter_dimension=0, tiled=True)]
    all_gather x1, blocking collectives: 24.4 us -> 38.8 us  [on_device(): all_active = lax.all_gather(active_total, 'dp', axis=0, tiled=True)]
    ppermute x0 -> x5, waiting for transfers between devices: none -> 7.46 us  [collected_by_bits(): theirs = lax.ppermute(blocks, axis, [(i, i ^ bit) for i in range(peers)])]
    ppermute x0 -> x5, starting transfers between devices: none -> 3.05 us  [collected_by_bits(): theirs = lax.ppermute(blocks, axis, [(i, i ^ bit) for i in range(peers)])]
  transfers between devices with their start and end apart: 5 -> 10, of which waited for: 2 -> 6; matrix products, arithmetic and copies ran while one was open for 19% -> 21% of each run, Pallas kernels for 0% -> 0%
where the time goes in v1:
time: 211 us; the launch traced here: 210 us
  blocking collectives  66.5 us (32%)
  waiting for transfers between devices  50.2 us (24%)
  matrix products  33.5 us (16%)
  other arithmetic  21.9 us (10%)
  between operations  20.9 us (10%)
  local copies, waits for them, and re-layouts  10.4 us (5%)
  starting transfers between devices  7.04 us (3%)
    all_gather x1, blocking collectives, on_device(): all_active = lax.all_gather(active_total, 'dp', axis=0, tiled=True)  38.8 us
    reduce_scatter x1, waiting for transfers between devices, on_device(): lax.psum_scatter(terms, 'fsdp', scatter_dimension=0, tiled=True)  22.6 us
    all_gather x1, blocking collectives, on_device(): group_img = lax.all_gather(img_b, 'fsdp', axis=0, tiled=True)  17.6 us
    reduce_scatter x1, waiting for transfers between devices, on_device(): lax.psum_scatter(text_part.astype(jnp.bfloat16), 'dp', scatter_dimension=...  10.2 us
    all_gather x1, blocking collectives, on_device(): column_txt = lax.all_gather(txt_b, 'dp', axis=0, tiled=True)  10.1 us
    all_gather x1, waiting for transfers between devices, on_device(): group_normed = lax.all_gather(normed, 'fsdp', axis=0, tiled=True)  9.79 us
    ppermute x5, waiting for transfers between devices, collected_by_bits(): theirs = lax.ppermute(blocks, axis, [(i, i ^ bit) for i in range(peers)])  7.46 us
    dot_general x1, matrix products, on_device(): row_down = jnp.dot(all_grad, w_down.T, preferred_element_type=jnp.float32)  6.54 us
  transfers between devices with their start and end apart: 10, of which 6 were waited for; matrix products, arithmetic and copies ran while one was open for 21% of the time, Pallas kernels for 0%

profile of v1, /device:TPU:0, one launch (start us, length us, event | category | flops | bytes accessed | tf_op | source)
XLA Modules:
  0.0 210.4 jit_solution(273732408413479940)
XLA Ops:
  8.0 1.5 fusion.167
  9.5 2.1 fusion.165
  11.6 1.9 fusion.166
  14.6 5.5 %fusion.163 = (f32[8,8]{1,0:T(8,128)S(1)}, f32[1,8,8,3072]{3,2,1,0:T(8,128)S(1)}) fusion(f32[3072]{0:T(1024)S(1)} %bitcast.150, f32[3072]{0:T(1024)S(1)} %bitcast.151, f32[3072]{0:T(1024)S(1)} %bitcast.154, f32[3072]{0:T(1024)S(1)} %bitcast.155, f32[3072]{0:T(1024)S(1)} %bitcast.156, f32[3072]{0:T(1024)S(1)} %bitcast.157, f32[3072]{0:T(1024)S(1)} %bitcast.158, ...), kind=kLoop, calls=%fused_computation.282 | loop fusion | flops 19267520 | bytes 2175232 | tf_op jit(solution)/shard_map/reduce_sum | solution.py:54
  23.5 17.6 %all_gather.15 = bf16[128,1152]{1,0:T(8,128)(2,1)S(1)} all-gather(bf16[32,1152]{1,0:T(8,128)(2,1)S(1)} %fusion.133), channel_id=1, replica_groups=mesh['dp'=8,'fsdp'=4] {'fsdp'}, dimensions={0}, use_global_device_ids=true | all-gather | bytes 368640 | tf_op jit(solution)/shard_map/all_gather | solution.py:131
  41.5 10.1 %all_gather.16 = bf16[256,1152]{1,0:T(8,128)(2,1)S(1)} all-gather(bf16[32,1152]{1,0:T(8,128)(2,1)S(1)} %fusion.134), channel_id=1, replica_groups=mesh['dp'=8,'fsdp'=4] {'dp'}, dimensions={0}, use_global_device_ids=true | all-gather | bytes 663552 | tf_op jit(solution)/shard_map/all_gather | solution.py:132
  53.6 9.8 %all-gather.4.cloned.1.call-done = bf16[256,3072]{1,0:T(8,128)(2,1)} async-done(((bf16[64,3072]{1,0:T(8,128)(2,1)}), bf16[256,3072]{1,0:T(8,128)(2,1)}) %all-gather.4.cloned.1.call-update) | async-done | bytes 1572880 | tf_op jit(solution)/shard_map/all_gather | solution.py:137
  63.4 6.0 %convert_reduce_fusion = (f32[4,1536]{1,0:T(4,128)S(1)}, f32[256,1536]{1,0:T(8,128)S(1)}) fusion(bf16[256,3072]{1,0:T(8,128)(2,1)} %all-gather.4.cloned.1.call-done, bf16[3072,1536]{1,0:T(8,128)(2,1)} %param.26), kind=kOutput, calls=%fused_computation.59 | convolution fusion | flops 2420238336 | bytes 12607488 | tf_op jit(solution)/shard_map/dot_general | solution.py:146
  69.4 5.0 %fusion.140 = f32[8,3072]{1,0:T(8,128)S(1)} fusion(bf16[1536,3072]{1,0:T(8,128)(2,1)} %param.27, bf16[4,1536]{1,0:T(4,128)(2,1)S(1)} %get-tuple-element.71, bf16[4,1536]{1,0:T(4,128)(2,1)S(1)} %get-tuple-element.70), kind=kOutput, calls=%fused_computation.226 | convolution fusion | flops 75546624 | bytes 9560064 | tf_op jit(solution)/shard_map/dot_general | solution.py:154
  75.6 1.9 fusion.7
  77.7 10.2 %reduce-scatter.5.cloned.1.call-done = bf16[32,1024]{1,0:T(8,128)(2,1)} async-done(((bf16[256,1024]{1,0:T(8,128)(2,1)}), bf16[32,1024]{1,0:T(8,128)(2,1)}) %reduce-scatter.5.cloned.1.call-update) | async-done | bytes 65552 | tf_op jit(solution)/shard_map/reduce_scatter | solution.py:197
  88.9 22.6 %reduce-scatter.3.cloned.1.call-done = bf16[48,1024]{1,0:T(8,128)(2,1)} async-done(((bf16[192,1024]{1,0:T(8,128)(2,1)}), bf16[48,1024]{1,0:T(8,128)(2,1)}) %reduce-scatter.3.cloned.1.call-update) | async-done | bytes 98320 | tf_op jit(solution)/shard_map/reduce_scatter | solution.py:166
  114.9 3.7 %fusion.168 = f32[1,1024]{1,0:T(1,128)S(1)} fusion(bf16[3072,1]{0,1:T(2,128)(2,1)S(1)} %reshape.361, bf16[3072,1024]{1,0:T(8,128)(2,1)} %param.31), kind=kOutput, calls=%fused_computation.286 | convolution fusion | flops 6291456 | bytes 6301696 | tf_op jit(solution)/shard_map/dot_general | solution.py:64
  121.3 4.6 %fusion.144 = f32[1,3072]{1,0:T(1,128)S(1)} fusion(bf16[3072,1024]{1,0:T(8,128)(2,1)} %param.31, f32[1,1024]{1,0:T(1,128)S(1)} %bitcast.195, f32[48,1024]{1,0:T(8,128)S(1)} %convert_element_type.101, f32[]{:T(128)S(6)} %sqrt.33), kind=kOutput, calls=%fused_computation.240 | convolution fusion | flops 6294528 | bytes 6311940 | tf_op jit(solution)/shard_map/dot_general | solution.py:67
  128.7 1.6 copy.47
  130.3 3.6 %all-to-all-start = ((bf16[256,8,384]{0,2,1:T(8,128)(2,1)}), bf16[256,8,384]{0,2,1:T(8,128)(2,1)S(1)}, u32[]{:S(2)}, u32[]{:S(2)}) async-start(bf16[256,8,384]{0,2,1:T(8,128)(2,1)} %bitcast.61), calls=%async_computation.2 | async-start | bytes 3145728 | tf_op jit(solution)/shard_map/all_to_all | solution.py:170
  134.7 1.3 collective-permute-start.1
  136.0 38.8 %all-gather = f32[8,4,1536]{2,1,0:T(4,128)S(1)} all-gather(f32[1,4,1536]{2,1,0:T(4,128)S(1)} %bitcast.135), channel_id=1, replica_groups=mesh['dp'=8,'fsdp'=4] {'dp'}, dimensions={0}, use_global_device_ids=true | all-gather | bytes 221184 | tf_op jit(solution)/shard_map/all_gather | solution.py:171
  177.2 3.3 %collective-permute-done.3 = bf16[8,1,3072]{2,0,1:T(8,128)(2,1)S(1)} collective-permute-done((bf16[8,1,3072]{2,0,1:T(8,128)(2,1)S(1)}, bf16[8,1,3072]{2,0,1:T(8,128)(2,1)S(1)}, u32[]{:S(2)}, u32[]{:S(2)}) %collective-permute-start.3) | collective-permute-done | bytes 49184 | tf_op jit(solution)/shard_map/ppermute | solution.py:21
  182.0 3.3 %collective-permute-done.4 = bf16[16,1,3072]{2,0,1:T(8,128)(2,1)S(1)} collective-permute-done((bf16[16,1,3072]{2,0,1:T(8,128)(2,1)S(1)}, bf16[16,1,3072]{2,0,1:T(8,128)(2,1)S(1)}, u32[]{:S(2)}, u32[]{:S(2)}) %collective-permute-start.4) | collective-permute-done | bytes 98336 | tf_op jit(solution)/shard_map/ppermute | solution.py:21
  185.4 1.9 fusion.121
  187.3 6.5 %fusion.169 = f32[32,1536]{1,0:T(8,128)S(1)} fusion(bf16[32,3072]{1,0:T(8,128)(2,1)S(1)} %bitcast.134, bf16[1536,3072]{1,0:T(8,128)(2,1)} %param.27), kind=kOutput, calls=%fused_computation.287 | convolution fusion | flops 301989888 | bytes 9830400 | tf_op jit(solution)/shard_map/dot_general | solution.py:176
  194.8 4.0 %fusion = bf16[2048,1536]{1,0:T(8,128)(2,1)S(1)} fusion(bf16[2048,1536]{1,0:T(8,128)(2,1)} %all-gather.6.cloned.1.call-done, f32[32,1536]{1,0:T(8,128)S(1)} %fusion.169), kind=kLoop, calls=%fused_computation.49 | loop fusion | flops 9437184 | bytes 12779520 | tf_op jit(solution)/shard_map/convert_element_type | solution.py:182
  198.8 4.1 %fusion.170 = f32[384,1536]{1,0:T(8,128)} fusion(bf16[2048,384]{1,0:T(8,128)(2,1)S(1)} %bitcast.129, bf16[2048,1536]{1,0:T(8,128)(2,1)S(1)} %fusion), kind=kOutput, calls=%fused_computation.288 | convolution fusion | flops 2415919104 | bytes 10223616 | tf_op jit(solution)/shard_map/dot_general | solution.py:185
  (114 shorter events, 18.5 us)
Async XLA Ops:
  8.0 55.4 %all-gather.4.cloned.1.call-start = ((), (), s32[]{:S(2)}) async-start(), calls=%async_computation.3 | async-start | bytes 1966080 | tf_op jit(solution)/shard_map/all_gather | solution.py:137
  14.6 6.0 %copy-start.8 = (f32[3072]{0:T(1024)S(1)}, f32[3072]{0:T(1024)}, u32[]{:S(2)}) copy-start(f32[3072]{0:T(1024)} %param.25) | copy-start | bytes 36868
  14.6 6.0 %copy-start.9 = (f32[3072]{0:T(1024)S(1)}, f32[3072]{0:T(1024)}, u32[]{:S(2)}) copy-start(f32[3072]{0:T(1024)} %param.24) | copy-start | bytes 36868
  20.1 2.8 %copy-start.2 = (bf16[32,1024]{1,0:T(8,128)(2,1)S(1)}, bf16[32,1024]{1,0:T(8,128)(2,1)}, u32[]{:S(2)}) copy-start(bf16[32,1024]{1,0:T(8,128)(2,1)} %param.16) | copy-start | bytes 196612
  20.1 2.9 %copy-start.11 = (s32[32]{0:T(128)S(1)}, s32[32]{0:T(128)}, u32[]{:S(2)}) copy-start(s32[32]{0:T(128)} %param.18) | copy-start | bytes 388
  20.1 2.9 %copy-start.12 = (s32[32]{0:T(128)S(1)}, s32[32]{0:T(128)}, u32[]{:S(2)}) copy-start(s32[32]{0:T(128)} %param.19) | copy-start | bytes 388
  20.2 21.0 %copy-start.3 = (bf16[32,1024]{1,0:T(8,128)(2,1)S(1)}, bf16[32,1024]{1,0:T(8,128)(2,1)}, u32[]{:S(2)}) copy-start(bf16[32,1024]{1,0:T(8,128)(2,1)} %param.17) | copy-start | bytes 196612
  21.5 66.4 %reduce-scatter.5.cloned.1.call-start = ((), (), s32[]{:S(2)}) async-start(), calls=%async_computation.5 | async-start | bytes 589824 | tf_op jit(solution)/shard_map/reduce_scatter | solution.py:197
  53.2 58.3 %reduce-scatter.3.cloned.1.call-start = ((), (), s32[]{:S(2)}) async-start(), calls=%async_computation.4 | async-start | bytes 491520 | tf_op jit(solution)/shard_map/reduce_scatter | solution.py:166
  75.4 119.4 %all-gather.6.cloned.1.call-start = ((), (), s32[]{:S(2)}) async-start(), calls=%async_computation.6 | async-start | bytes 7077888 | tf_op jit(solution)/shard_map/all_gather | solution.py:169
  75.6 2.0 copy-start.1
  75.6 36.7 %copy-start.7 = (f32[3072]{0:T(1024)S(1)}, f32[3072]{0:T(1024)}, u32[]{:S(2)}) copy-start(f32[3072]{0:T(1024)} %param.28) | copy-start | bytes 36868
  75.6 39.2 %copy-start.6 = (f32[3072]{0:T(1024)S(1)}, f32[3072]{0:T(1024)}, u32[]{:S(2)}) copy-start(f32[3072]{0:T(1024)} %param.29) | copy-start | bytes 36868
  75.6 39.2 %copy-start.10 = (f32[3072]{0:T(1024)S(1)}, f32[3072]{0:T(1024)}, u32[]{:S(2)}) copy-start(f32[3072]{0:T(1024)} %param.30) | copy-start | bytes 36868
  114.9 5.1 %copy-start.5 = (bf16[48,1024]{1,0:T(8,128)(2,1)S(1)}, bf16[48,1024]{1,0:T(8,128)(2,1)}, u32[]{:S(2)}) copy-start(bf16[48,1024]{1,0:T(8,128)(2,1)} %reduce-scatter.3.cloned.1.call-done) | copy-start | bytes 294916
  121.3 6.7 %copy-start.4 = (bf16[32,1024]{1,0:T(8,128)(2,1)S(1)}, bf16[32,1024]{1,0:T(8,128)(2,1)}, u32[]{:S(2)}) copy-start(bf16[32,1024]{1,0:T(8,128)(2,1)} %reduce-scatter.5.cloned.1.call-done) | copy-start | bytes 196612
  121.3 7.4 %copy-start = (bf16[256,3072]{1,0:T(8,128)(2,1)S(1)}, bf16[256,3072]{1,0:T(8,128)(2,1)}, u32[]{:S(2)}) copy-start(bf16[256,3072]{1,0:T(8,128)(2,1)} %all-gather.4.cloned.1.call-done) | copy-start | bytes 4718596
  127.9 6.1 %collective-permute-start = (bf16[1,1,3072]{2,1,0:T(2,128)(2,1)S(1)}, bf16[1,1,3072]{2,1,0:T(2,128)(2,1)S(1)}, u32[]{:S(2)}, u32[]{:S(2)}) collective-permute-start(bf16[1,1,3072]{2,1,0:T(2,128)(2,1)S(1)} %broadcast_in_dim.15), channel_id=1, source_target_pairs={{0,1},{1,0},{2,3},{3,2},{4,5},{5,4},{6,7},{7,6},{8,9},{9,8},{10,11... | collective-permute-start | bytes 18440 | tf_op jit(solution)/shard_map/ppermute | solution.py:21
  130.3 63.6 %all-to-all-start = ((bf16[256,8,384]{0,2,1:T(8,128)(2,1)}), bf16[256,8,384]{0,2,1:T(8,128)(2,1)S(1)}, u32[]{:S(2)}, u32[]{:S(2)}) async-start(bf16[256,8,384]{0,2,1:T(8,128)(2,1)} %bitcast.61), calls=%async_computation.2 | async-start | bytes 3145728 | tf_op jit(solution)/shard_map/all_to_all | solution.py:170
  134.7 40.3 %collective-permute-start.1 = (bf16[2,1,3072]{2,0,1:T(2,128)(2,1)S(1)}, bf16[2,1,3072]{2,0,1:T(2,128)(2,1)S(1)}, u32[]{:S(2)}, u32[]{:S(2)}) collective-permute-start(bf16[2,1,3072]{2,0,1:T(2,128)(2,1)S(1)} %get-tuple-element.69), channel_id=1, source_target_pairs={{0,2},{1,3},{2,0},{3,1},{4,6},{5,7},{6,4},{7,5},{8,10},{9,11},{10,... | collective-permute-start | bytes 36872 | tf_op jit(solution)/shard_map/ppermute | solution.py:21
  175.1 1.3 collective-permute-start.2
  176.4 4.2 %collective-permute-start.3 = (bf16[8,1,3072]{2,0,1:T(8,128)(2,1)S(1)}, bf16[8,1,3072]{2,0,1:T(8,128)(2,1)S(1)}, u32[]{:S(2)}, u32[]{:S(2)}) collective-permute-start(bf16[8,1,3072]{2,0,1:T(8,128)(2,1)S(1)} %reshape.355), channel_id=1, source_target_pairs={{0,8},{1,9},{2,10},{3,11},{4,12},{5,13},{6,14},{7,15},{8,0},{9,1},... | collective-permute-start | bytes 147464 | tf_op jit(solution)/shard_map/ppermute | solution.py:21
  180.6 4.7 %collective-permute-start.4 = (bf16[16,1,3072]{2,0,1:T(8,128)(2,1)S(1)}, bf16[16,1,3072]{2,0,1:T(8,128)(2,1)S(1)}, u32[]{:S(2)}, u32[]{:S(2)}) collective-permute-start(bf16[16,1,3072]{2,0,1:T(8,128)(2,1)S(1)} %get-tuple-element.67), channel_id=1, source_target_pairs={{0,16},{1,17},{2,18},{3,19},{4,20},{5,21},{6,22},{7,23},{8,24},{9,... | collective-permute-start | bytes 294920 | tf_op jit(solution)/shard_map/ppermute | solution.py:21
Sparse Core Ops, SparseCore 0:
  21.7 41.7 all-gather.3
Sparse Core Ops, SparseCore 1:
  53.3 34.5 reduce-scatter.4
  90.6 20.9 reduce-scatter.2
  113.3 59.4 all-gather.5
